TPU v7x, 32 devices: a whole 2x2x4 slice. The times are simulated.
32 devices in a mesh: groups: 2 (over y), row: 16 (over z, x, core).
Axes of the slice: x: 2, y: 2, z: 4, core: 2. Of those that a mesh axis runs over, the one named last changes fastest.
Arguments:
- layer_input: bfloat16 [8192, 512], P('row', 'groups'), parts along dimension 1, may hold values from -6 to 6
- output_grad: bfloat16 [8192, 512], P('row', 'groups'), parts along dimension 1, may hold values from -1.5 to 1.5
- gate_weight: bfloat16 [28672, 8192], P(('groups', 'row')), parts along dimension 0, may hold values from -0.09375 to 0.09375
- up_weight: bfloat16 [28672, 8192], P(('groups', 'row')), parts along dimension 0, may hold values from -0.09375 to 0.09375
- down_weight: bfloat16 [28672, 8192], P(('groups', 'row')), parts along dimension 0, may hold values from -0.046875 to 0.046875
Outputs:
- input_grad: bfloat16 [8192, 512], P('row', 'groups'), parts along dimension 1
- gate_grad: bfloat16 [28672, 8192], P(('groups', 'row')), parts along dimension 0
- up_grad: bfloat16 [28672, 8192], P(('groups', 'row')), parts along dimension 0
- down_grad: bfloat16 [28672, 8192], P(('groups', 'row')), parts along dimension 0
There are 2 independent parts, one for each index of `groups`. A program takes and returns all parts, laid end to end along the dimension named above; each array names one. Nothing has to cross between parts.
All inputs are finite; a program needn't handle non-finite values.
Results may differ from a plain program's by a relative error of at most 0.0049.
Values may be sent and summed in bfloat16 or wider, within the bound.
A program may use at most 192 MiB of HBM per device.

v0:
```python
import jax
import jax.numpy as jnp
from jax import lax
from jax.sharding import PartitionSpec as P


def over_tokens(first_mat, second_mat):
    return lax.dot_general(
        first_mat, second_mat, (((1,), (1,)), ((), ())), preferred_element_type=jnp.float32
    )


def over_hidden(first_mat, second_mat):
    return lax.dot_general(
        first_mat, second_mat, (((0,), (0,)), ((), ())), preferred_element_type=jnp.float32
    )


def activation_parts(gate_pre, up_pre):
    sig = jax.nn.sigmoid(gate_pre)
    act = gate_pre * sig
    hidden_act = (act * up_pre).astype(jnp.bfloat16)
    return (sig, act, hidden_act)


def pre_grads(hidden_grad, gate_pre, up_pre, sig, act):
    grad_gate_pre = (hidden_grad * up_pre * sig * (1.0 + gate_pre * (1.0 - sig))).astype(
        jnp.bfloat16
    )
    grad_up_pre = (hidden_grad * act).astype(jnp.bfloat16)
    return (grad_gate_pre, grad_up_pre)


def on_device(layer_input, output_grad, gate_weight, up_weight, down_weight):
    block_in = lax.all_gather(layer_input, "row", axis=0, tiled=True)
    gate_pre = jnp.dot(gate_weight, block_in, preferred_element_type=jnp.float32)
    up_pre = jnp.dot(up_weight, block_in, preferred_element_type=jnp.float32)
    sig, act, hidden_act = activation_parts(gate_pre, up_pre)
    block_in = lax.all_gather(output_grad, "row", axis=0, tiled=True)
    grad_new = jnp.dot(down_weight, block_in, preferred_element_type=jnp.float32)
    grad_block = over_tokens(hidden_act, block_in).astype(jnp.bfloat16)
    grad_gate_pre, grad_up_pre = pre_grads(grad_new, gate_pre, up_pre, sig, act)
    block_in = lax.all_gather(layer_input, "row", axis=0, tiled=True)
    gate_grad = over_tokens(grad_gate_pre, block_in).astype(jnp.bfloat16)
    up_grad = over_tokens(grad_up_pre, block_in).astype(jnp.bfloat16)
    terms = over_hidden(gate_weight, grad_gate_pre) + over_hidden(up_weight, grad_up_pre)
    input_grad = lax.psum_scatter(terms, "row", scatter_dimension=0, tiled=True).astype(
        jnp.bfloat16
    )
    return (input_grad, gate_grad, up_grad, grad_block)


def solution(mesh):
    return jax.shard_map(
        on_device,
        mesh=mesh,
        in_specs=(
            P("row", "groups"),
            P("row", "groups"),
            P(("groups", "row"), None),
            P(("groups", "row"), None),
            P(("groups", "row"), None),
        ),
        out_specs=(
            P("row", "groups"),
            P(("groups", "row"), None),
            P(("groups", "row"), None),
            P(("groups", "row"), None),
        ),
        check_vma=False,
    )
```

profile of v0, /device:TPU:0, one launch (start us, length us, event | category | flops | bytes accessed | tf_op | source)
XLA Modules:
  0.0 256.2 jit_solution(9589781873817059000)
XLA Ops:
  7.2 0.0 all-gather.5.cloned.1.call-start
  7.2 0.7 all-gather.5.cloned.1.call-update
  7.9 0.0 all-gather.3.cloned.1.call-start
  7.9 0.7 all-gather.3.cloned.1.call-update
  8.6 0.0 reduce-scatter.2.cloned.1.call-start
  8.7 54.6 %all-gather.5.cloned.1.call-done = bf16[8192,256]{1,0:T(8,128)(2,1)} async-done(((bf16[512,256]{1,0:T(8,128)(2,1)}), bf16[8192,256]{1,0:T(8,128)(2,1)}) %all-gather.5.cloned.1.call-update) | async-done | bytes 4194320 | tf_op jit(solution)/shard_map/all_gather | solution.py:35
  63.3 0.0 copy-start
  63.3 0.0 copy-start.1
  63.3 8.6 %fusion.5 = f32[896,256]{1,0:T(8,128)S(1)} fusion(bf16[896,8192]{1,0:T(8,128)(2,1)} %param.7, bf16[8192,256]{1,0:T(8,128)(2,1)} %all-gather.5.cloned.1.call-done), kind=kOutput, calls=%fused_computation.12 | convolution fusion | flops 3758096384 | bytes 19791872 | tf_op jit(solution)/shard_map/dot_general | solution.py:36
  71.9 2.2 copy-done
  74.1 1.2 copy-done.1
  75.3 3.9 %fusion.4 = f32[896,256]{1,0:T(8,128)S(1)} fusion(bf16[896,8192]{1,0:T(8,128)(2,1)S(1)} %copy-done, bf16[8192,256]{1,0:T(8,128)(2,1)S(1)} %copy-done.1), kind=kOutput, calls=%fused_computation.11 | convolution fusion | flops 3758096384 | bytes 19791872 | tf_op jit(solution)/shard_map/dot_general | solution.py:37
  79.2 35.1 %all-gather.3.cloned.1.call-done = bf16[8192,256]{1,0:T(8,128)(2,1)} async-done(((bf16[512,256]{1,0:T(8,128)(2,1)}), bf16[8192,256]{1,0:T(8,128)(2,1)}) %all-gather.3.cloned.1.call-update) | async-done | bytes 4194320 | tf_op jit(solution)/shard_map/all_gather | solution.py:39
  114.4 10.5 %multiply_convert_fusion.1 = (bf16[896,256]{1,0:T(8,128)(2,1)S(1)}, bf16[896,256]{1,0:T(8,128)(2,1)S(1)}) fusion(f32[896,256]{1,0:T(8,128)S(1)} %fusion.5, f32[896,256]{1,0:T(8,128)S(1)} %fusion.4, bf16[896,8192]{1,0:T(8,128)(2,1)} %param.9, bf16[8192,256]{1,0:T(8,128)(2,1)} %all-gather.3.cloned.1.call-done), kind=kOutput, calls=%fused_computation.6 | convolution fusion | flops 3761078272 | bytes 21626880 | tf_op jit(solution)/shard_map/dot_general | solution.py:40
  124.9 8.0 %fusion.6 = f32[256,8192]{1,0:T(8,128)S(1)} fusion(bf16[896,256]{1,0:T(8,128)(2,1)S(1)} %get-tuple-element.9, bf16[896,8192]{1,0:T(8,128)(2,1)} %param.7), kind=kOutput, calls=%fused_computation.13 | convolution fusion | flops 3758096384 | bytes 23527424 | tf_op jit(solution)/shard_map/dot_general | solution.py:14
  132.9 12.5 %fusion = f32[8192,256]{0,1:T(8,128)} fusion(f32[256,8192]{1,0:T(8,128)S(1)} %fusion.6, bf16[896,256]{1,0:T(8,128)(2,1)S(1)} %get-tuple-element.8, bf16[896,8192]{1,0:T(8,128)(2,1)} %param.8), kind=kOutput, calls=%fused_computation.4 | convolution fusion | flops 3760193536 | bytes 31916032 | tf_op jit(solution)/shard_map/dot_general | solution.py:14
  145.4 0.0 reduce-scatter.2.cloned.1.call-update
  145.5 10.4 %convolution_convert_fusion.1 = bf16[896,8192]{1,0:T(8,128)(2,1)} fusion(bf16[896,256]{1,0:T(8,128)(2,1)S(1)} %get-tuple-element.8, bf16[8192,256]{1,0:T(8,128)(2,1)} %all-gather.5.cloned.1.call-done), kind=kOutput, calls=%fused_computation.1 | convolution fusion | flops 3765436416 | bytes 19333120 | tf_op jit(solution)/shard_map/dot_general | solution.py:8
  155.9 10.6 %convolution_convert_fusion.2 = bf16[896,8192]{1,0:T(8,128)(2,1)} fusion(bf16[896,256]{1,0:T(8,128)(2,1)S(1)} %get-tuple-element.9, bf16[8192,256]{1,0:T(8,128)(2,1)} %all-gather.5.cloned.1.call-done), kind=kOutput, calls=%fused_computation.2 | convolution fusion | flops 3765436416 | bytes 19333120 | tf_op jit(solution)/shard_map/dot_general | solution.py:8
  166.5 9.8 %convolution_convert_fusion = bf16[896,8192]{1,0:T(8,128)(2,1)} fusion(bf16[8192,256]{1,0:T(8,128)(2,1)} %all-gather.3.cloned.1.call-done, f32[896,256]{1,0:T(8,128)S(1)} %fusion.4, f32[896,256]{1,0:T(8,128)S(1)} %fusion.5), kind=kOutput, calls=%fused_computation | convolution fusion | flops 3766812672 | bytes 20709376 | tf_op jit(solution)/shard_map/dot_general | solution.py:8
  176.4 71.4 %reduce-scatter.2.cloned.1.call-done = f32[512,256]{0,1:T(8,128)} async-done(((f32[8192,256]{0,1:T(8,128)}), f32[512,256]{0,1:T(8,128)}) %reduce-scatter.2.cloned.1.call-update) | async-done | bytes 524304 | tf_op jit(solution)/shard_map/reduce_scatter | solution.py:47
  247.8 1.1 convert_element_type.23
  248.9 0.8 copy.9
Async XLA Ops:
  7.2 56.1 %all-gather.5.cloned.1.call-start = ((), (), s32[]{:S(2)}) async-start(), calls=%async_computation.2 | async-start | bytes 4456448 | tf_op jit(solution)/shard_map/all_gather | solution.py:35
  7.9 106.5 %all-gather.3.cloned.1.call-start = ((), (), s32[]{:S(2)}) async-start(), calls=%async_computation.1 | async-start | bytes 4456448 | tf_op jit(solution)/shard_map/all_gather | solution.py:39
  8.6 239.1 %reduce-scatter.2.cloned.1.call-start = ((), (), s32[]{:S(2)}) async-start(), calls=%async_computation.3 | async-start | bytes 8912896 | tf_op jit(solution)/shard_map/reduce_scatter | solution.py:47
  63.3 10.8 %copy-start = (bf16[896,8192]{1,0:T(8,128)(2,1)S(1)}, bf16[896,8192]{1,0:T(8,128)(2,1)}, u32[]{:S(2)}) copy-start(bf16[896,8192]{1,0:T(8,128)(2,1)} %param.8) | copy-start | bytes 44040196
  63.3 12.0 %copy-start.1 = (bf16[8192,256]{1,0:T(8,128)(2,1)S(1)}, bf16[8192,256]{1,0:T(8,128)(2,1)}, u32[]{:S(2)}) copy-start(bf16[8192,256]{1,0:T(8,128)(2,1)} %all-gather.5.cloned.1.call-done) | copy-start | bytes 12582916
Sparse Core Ops, SparseCore 0:
  10.1 53.0 all-gather.4
  65.4 48.8 all-gather.2
  145.6 102.1 reduce-scatter.1
where the time goes:
time: 257 us; the launch traced here: 256 us
  waiting for transfers between devices  163 us (63%)
  matrix products  74.5 us (29%)
  between operations  13.8 us (5%)
  local copies, waits for them, and re-layouts  4.25 us (2%)
    reduce_scatter x1, waiting for transfers between devices, on_device(): lax.psum_scatter(terms, 'row', scatter_dimension=0, tiled=True)  71.4 us
    all_gather x1, waiting for transfers between devices, on_device(): block_in = lax.all_gather(layer_input, 'row', axis=0, tiled=True)  54.6 us
    all_gather x1, waiting for transfers between devices, on_device(): block_in = lax.all_gather(output_grad, 'row', axis=0, tiled=True)  35.1 us
    dot_general x3, matrix products, over_tokens(): lax.dot_general(first_mat, second_mat, (((1,), (1,)), ((), ())), preferre...  30.9 us
    dot_general x2, matrix products, over_hidden(): lax.dot_general(first_mat, second_mat, (((0,), (0,)), ((), ())), preferre...  20.6 us
    dot_general x1, matrix products, on_device(): jnp.dot(down_weight, block_in, preferred_element_type=jnp.float32)  10.5 us
    dot_general x1, matrix products, on_device(): jnp.dot(gate_weight, block_in, preferred_element_type=jnp.float32)  8.59 us
  transfers between devices with their start and end apart: 3, of which 3 were waited for; matrix products, arithmetic and copies ran while one was open for 17% of the time, Pallas kernels for 0%

commit v1 on v0

--- a/solution.py
+++ b/solution.py
@@ -32,7 +32,10 @@
 
 
 def on_device(layer_input, output_grad, gate_weight, up_weight, down_weight):
-    block_in = lax.all_gather(layer_input, "row", axis=0, tiled=True)
+    count = lax.axis_size("row")
+    blocks = jnp.stack([layer_input for _ in range(count)])
+    blocks = lax.all_to_all(blocks, "row", split_axis=0, concat_axis=0)
+    block_in = jnp.concatenate(blocks, axis=0)
     gate_pre = jnp.dot(gate_weight, block_in, preferred_element_type=jnp.float32)
     up_pre = jnp.dot(up_weight, block_in, preferred_element_type=jnp.float32)
     sig, act, hidden_act = activation_parts(gate_pre, up_pre)

time: 257 us -> 307 us (1.19)
  waiting for transfers between devices: 163 us -> 201 us
  starting transfers between devices: 0.11 us -> 7.68 us
  matrix products: 74.5 us -> 77.6 us
    all_to_all x0 -> x1, waiting for transfers between devices: none -> 102 us  [on_device(): blocks = lax.all_to_all(blocks, 'row', split_axis=0, concat_axis=0)]
    all_gather x1, waiting for transfers between devices: 54.6 us -> 3.47 us  [on_device(): block_in = lax.all_gather(layer_input, 'row', axis=0, tiled=True)]
    all_gather x1, waiting for transfers between devices: 35.1 us -> 0.01 us  [on_device(): block_in = lax.all_gather(output_grad, 'row', axis=0, tiled=True)]
    reduce_scatter x1, waiting for transfers between devices: 71.4 us -> 93.7 us  [on_device(): lax.psum_scatter(terms, 'row', scatter_dimension=0, tiled=True)]
    all_to_all x0 -> x1, starting transfers between devices: none -> 7.57 us  [on_device(): blocks = lax.all_to_all(blocks, 'row', split_axis=0, concat_axis=0)]
    another operation x0 -> x1, local copies, waits for them, and re-layouts: none -> 3.37 us  [on_device(): blocks = jnp.stack([layer_input for _ in range(count)])]
    dot_general x1, matrix products: 3.94 us -> 7.05 us  [on_device(): up_pre = jnp.dot(up_weight, block_in, preferred_element_type=jnp.float32)]
  transfers between devices with their start and end apart: 3 -> 4, of which waited for: 3 -> 3; matrix products, arithmetic and copies ran while one was open for 17% -> 26% of each run, Pallas kernels for 0% -> 0%
where the time goes in v1:
time: 307 us
  waiting for transfers between devices  201 us (65%)
  matrix products  77.6 us (25%)
  between operations  13.8 us (4%)
  starting transfers between devices  7.68 us (3%)
  local copies, waits for them, and re-layouts  5.9 us (2%)
    all_to_all x1, waiting for transfers between devices, on_device(): blocks = lax.all_to_all(blocks, 'row', split_axis=0, concat_axis=0)  102 us
    reduce_scatter x1, waiting for transfers between devices, on_device(): lax.psum_scatter(terms, 'row', scatter_dimension=0, tiled=True)  93.7 us
    dot_general x3, matrix products, over_tokens(): lax.dot_general(first_mat, second_mat, (((1,), (1,)), ((), ())), preferre...  29.9 us
    dot_general x2, matrix products, over_hidden(): lax.dot_general(first_mat, second_mat, (((0,), (0,)), ((), ())), preferre...  21.2 us
    dot_general x1, matrix products, on_device(): jnp.dot(down_weight, block_in, preferred_element_type=jnp.float32)  10.8 us
    dot_general x1, matrix products, on_device(): jnp.dot(gate_weight, block_in, preferred_element_type=jnp.float32)  8.6 us
    all_to_all x1, starting transfers between devices, on_device(): blocks = lax.all_to_all(blocks, 'row', split_axis=0, concat_axis=0)  7.57 us
    dot_general x1, matrix products, on_device(): up_pre = jnp.dot(up_weight, block_in, preferred_element_type=jnp.float32)  7.05 us
  transfers between devices with their start and end apart: 4, of which 3 were waited for; matrix products, arithmetic and copies ran while one was open for 26% of the time, Pallas kernels for 0%

profile of v1, /device:TPU:0, one launch (start us, length us, event | category | flops | bytes accessed | tf_op | source)
XLA Modules:
  0.0 306.6 jit_solution(17568805911509957434)
XLA Ops:
  7.2 0.0 all-gather.3.cloned.1.call-start
  7.2 0.7 all-gather.3.cloned.1.call-update
  7.9 3.4 %stack.2 = bf16[16,512,256]{2,1,0:T(8,128)(2,1)} broadcast(bf16[512,256]{1,0:T(8,128)(2,1)} %param.5), dimensions={1,2} | broadcast | bytes 4456448 | tf_op jit(solution)/shard_map/stack | solution.py:36
  11.3 0.0 slice-start
  11.3 7.6 %all-to-all-start = ((bf16[16,512,256]{2,1,0:T(8,128)(2,1)}), bf16[16,512,256]{2,1,0:T(8,128)(2,1)}, u32[]{:S(2)}, u32[]{:S(2)}) async-start(bf16[16,512,256]{2,1,0:T(8,128)(2,1)} %stack.2), calls=%async_computation | async-start | bytes 8388608 | tf_op jit(solution)/shard_map/all_to_all | solution.py:37
  18.8 0.0 all-gather.5.cloned.1.call-start
  18.9 0.7 all-gather.5.cloned.1.call-update
  19.6 0.0 reduce-scatter.2.cloned.1.call-start
  19.6 102.0 %all-to-all-done = bf16[16,512,256]{2,1,0:T(8,128)(2,1)} async-done(((bf16[16,512,256]{2,1,0:T(8,128)(2,1)}), bf16[16,512,256]{2,1,0:T(8,128)(2,1)}, u32[]{:S(2)}, u32[]{:S(2)}) %all-to-all-start) | async-done | bytes 4194336 | tf_op jit(solution)/shard_map/all_to_all | solution.py:37
  121.6 0.0 slice-start.1
  121.6 0.0 slice-start.2
  121.6 0.0 slice-start.3
  121.6 8.6 %fusion.5 = f32[896,256]{1,0:T(8,128)S(1)} fusion(bf16[896,8192]{1,0:T(8,128)(2,1)} %param.7, bf16[8192,256]{1,0:T(8,128)(2,1)} %bitcast), kind=kOutput, calls=%fused_computation.12 | convolution fusion | flops 3758096384 | bytes 19791872 | tf_op jit(solution)/shard_map/dot_general | solution.py:39
  130.2 0.0 slice-done
  130.2 0.0 slice-done.1
  130.3 0.4 slice-done.2
  130.6 1.3 slice-done.3
  131.9 7.1 %fusion.4 = f32[896,256]{1,0:T(8,128)} fusion(bf16[896,8192]{1,0:T(8,128)(2,1)S(1)} %bitcast.19, bf16[8192,256]{1,0:T(8,128)(2,1)} %bitcast), kind=kOutput, calls=%fused_computation.11 | convolution fusion | flops 3758096384 | bytes 19791872 | tf_op jit(solution)/shard_map/dot_general | solution.py:40
  139.0 0.0 all-gather.3.cloned.1.call-done
  139.0 10.8 %multiply_convert_fusion.1 = (bf16[896,256]{1,0:T(8,128)(2,1)S(1)}, bf16[896,256]{1,0:T(8,128)(2,1)S(1)}) fusion(f32[896,256]{1,0:T(8,128)S(1)} %fusion.5, f32[896,256]{1,0:T(8,128)} %fusion.4, bf16[896,8192]{1,0:T(8,128)(2,1)} %param.9, bf16[8192,256]{1,0:T(8,128)(2,1)} %all-gather.3.cloned.1.call-done), kind=kOutput, calls=%fused_computation.6 | convolution fusion | flops 3761078272 | bytes 21626880 | tf_op jit(solution)/shard_map/dot_general | solution.py:43
  149.8 8.6 %fusion.6 = f32[256,8192]{1,0:T(8,128)S(1)} fusion(bf16[896,256]{1,0:T(8,128)(2,1)S(1)} %get-tuple-element.9, bf16[896,8192]{1,0:T(8,128)(2,1)} %param.7), kind=kOutput, calls=%fused_computation.13 | convolution fusion | flops 3758096384 | bytes 23527424 | tf_op jit(solution)/shard_map/dot_general | solution.py:14
  158.4 12.6 %fusion = f32[8192,256]{0,1:T(8,128)} fusion(f32[256,8192]{1,0:T(8,128)S(1)} %fusion.6, bf16[896,256]{1,0:T(8,128)(2,1)S(1)} %get-tuple-element.8, bf16[896,8192]{1,0:T(8,128)(2,1)} %param.8), kind=kOutput, calls=%fused_computation.4 | convolution fusion | flops 3760193536 | bytes 31916032 | tf_op jit(solution)/shard_map/dot_general | solution.py:14
  171.0 0.0 reduce-scatter.2.cloned.1.call-update
  171.0 3.5 %all-gather.5.cloned.1.call-done = bf16[8192,256]{1,0:T(8,128)(2,1)} async-done(((bf16[512,256]{1,0:T(8,128)(2,1)}), bf16[8192,256]{1,0:T(8,128)(2,1)}) %all-gather.5.cloned.1.call-update) | async-done | bytes 4194320 | tf_op jit(solution)/shard_map/all_gather | solution.py:46
  174.5 9.8 %convolution_convert_fusion.1 = bf16[896,8192]{1,0:T(8,128)(2,1)} fusion(bf16[896,256]{1,0:T(8,128)(2,1)S(1)} %get-tuple-element.8, bf16[8192,256]{1,0:T(8,128)(2,1)} %all-gather.5.cloned.1.call-done), kind=kOutput, calls=%fused_computation.1 | convolution fusion | flops 3765436416 | bytes 19333120 | tf_op jit(solution)/shard_map/dot_general | solution.py:8
  184.2 0.0 copy-start
  184.2 9.8 %convolution_convert_fusion.2 = bf16[896,8192]{1,0:T(8,128)(2,1)} fusion(bf16[896,256]{1,0:T(8,128)(2,1)S(1)} %get-tuple-element.9, bf16[8192,256]{1,0:T(8,128)(2,1)} %all-gather.5.cloned.1.call-done), kind=kOutput, calls=%fused_computation.2 | convolution fusion | flops 3765436416 | bytes 19333120 | tf_op jit(solution)/shard_map/dot_general | solution.py:8
  194.1 0.0 copy-done
  194.1 10.3 %convolution_convert_fusion = bf16[896,8192]{1,0:T(8,128)(2,1)} fusion(bf16[8192,256]{1,0:T(8,128)(2,1)} %all-gather.3.cloned.1.call-done, f32[896,256]{1,0:T(8,128)S(1)} %copy-done, f32[896,256]{1,0:T(8,128)S(1)} %fusion.5), kind=kOutput, calls=%fused_computation | convolution fusion | flops 3766812672 | bytes 20709376 | tf_op jit(solution)/shard_map/dot_general | solution.py:8
  204.4 93.7 %reduce-scatter.2.cloned.1.call-done = f32[512,256]{0,1:T(8,128)} async-done(((f32[8192,256]{0,1:T(8,128)}), f32[512,256]{0,1:T(8,128)}) %reduce-scatter.2.cloned.1.call-update) | async-done | bytes 524304 | tf_op jit(solution)/shard_map/reduce_scatter | solution.py:50
  298.1 1.1 convert_element_type.23
  299.2 0.8 copy.9
  (1 shorter events, 0.0 us)
Async XLA Ops:
  7.2 131.8 %all-gather.3.cloned.1.call-start = ((), (), s32[]{:S(2)}) async-start(), calls=%async_computation.2 | async-start | bytes 4456448 | tf_op jit(solution)/shard_map/all_gather | solution.py:42
  11.3 119.0 %slice-start = ((s8[14680064]{0:T(1024)(128)(4,1)}), s8[2097152]{0:T(1024)(128)(4,1)S(1)}, s32[]{:S(2)}) async-start(s8[14680064]{0:T(1024)(128)(4,1)} %bitcast.18), calls=%async_computation.5 | async-start | bytes 4194304
  11.3 110.4 %all-to-all-start = ((bf16[16,512,256]{2,1,0:T(8,128)(2,1)}), bf16[16,512,256]{2,1,0:T(8,128)(2,1)}, u32[]{:S(2)}, u32[]{:S(2)}) async-start(bf16[16,512,256]{2,1,0:T(8,128)(2,1)} %stack.2), calls=%async_computation | async-start | bytes 8388608 | tf_op jit(solution)/shard_map/all_to_all | solution.py:37
  18.8 155.6 %all-gather.5.cloned.1.call-start = ((), (), s32[]{:S(2)}) async-start(), calls=%async_computation.4 | async-start | bytes 4456448 | tf_op jit(solution)/shard_map/all_gather | solution.py:46
  19.6 278.5 %reduce-scatter.2.cloned.1.call-start = ((), (), s32[]{:S(2)}) async-start(), calls=%async_computation.3 | async-start | bytes 8912896 | tf_op jit(solution)/shard_map/reduce_scatter | solution.py:50
  121.6 8.6 %slice-start.1 = ((s8[14680064]{0:T(1024)(128)(4,1)}), s8[4194304]{0:T(1024)(128)(4,1)S(1)}, s32[]{:S(2)}) async-start(s8[14680064]{0:T(1024)(128)(4,1)} %bitcast.18), calls=%async_computation.6 | async-start | bytes 8388608
  121.6 9.0 %slice-start.2 = ((s8[14680064]{0:T(1024)(128)(4,1)}), s8[4194304]{0:T(1024)(128)(4,1)S(1)}, s32[]{:S(2)}) async-start(s8[14680064]{0:T(1024)(128)(4,1)} %bitcast.18), calls=%async_computation.7 | async-start | bytes 8388608
  121.6 10.3 %slice-start.3 = ((s8[14680064]{0:T(1024)(128)(4,1)}), s8[4194304]{0:T(1024)(128)(4,1)S(1)}, s32[]{:S(2)}) async-start(s8[14680064]{0:T(1024)(128)(4,1)} %bitcast.18), calls=%async_computation.8 | async-start | bytes 8388608
  184.2 9.8 %copy-start = (f32[896,256]{1,0:T(8,128)S(1)}, f32[896,256]{1,0:T(8,128)}, u32[]{:S(2)}) copy-start(f32[896,256]{1,0:T(8,128)} %fusion.4) | copy-start | bytes 2752516
Sparse Core Ops, SparseCore 0:
  10.1 105.3 all-gather.2
  117.6 56.7 all-gather.4
  178.6 119.5 reduce-scatter.1
